TPU v7x, 32 devices: a whole 2x2x4 slice. The times are simulated.
32 devices in a mesh: dp: 8 (over z, y), tensor: 4 (over x, core).
Axes of the slice: x: 2, y: 2, z: 4, core: 2. Of those that a mesh axis runs over, the one named last changes fastest.
Arguments:
- inputs: bfloat16 [4096, 512], P('dp'), may hold values from -6 to 6
- query_weight: bfloat16 [512, 512], P(None, 'tensor'), may hold values from -0.25 to 0.25
- key_weight: bfloat16 [512, 512], P(None, 'tensor'), may hold values from -0.25 to 0.25
- value_weight: bfloat16 [512, 512], P(None, 'tensor'), may hold values from -0.25 to 0.25
- query_bias: float32 [512], P('tensor'), may hold values from -3 to 3
- value_bias: float32 [512], P('tensor'), may hold values from -3 to 3
- position_bias: float32 [49, 16], P(None, 'tensor'), may hold values from -4 to 4
- proj_weight: bfloat16 [512, 512], P('tensor'), may hold values from -0.5 to 0.5
- proj_bias: float32 [512], replicated, may hold values from -2 to 2
- norm1_gain: float32 [512], replicated, may hold values from 0.5 to 1.5
- norm1_shift: float32 [512], replicated, may hold values from -2 to 2
- norm2_gain: float32 [512], replicated, may hold values from 0.5 to 1.5
- norm2_shift: float32 [512], replicated, may hold values from -2 to 2
- up_weight: bfloat16 [512, 2048], P(None, 'tensor'), may hold values from -0.25 to 0.25
- up_bias: float32 [2048], P('tensor'), may hold values from -2 to 2
- down_weight: bfloat16 [2048, 512], P('tensor'), may hold values from -0.25 to 0.25
- down_bias: float32 [512], replicated, may hold values from -2 to 2
- segment_ids: int32 [8, 512], P('dp'), may hold values from 0 to 3, never falling along the last dimension, each value on 1 to 256 neighbouring positions
- valid_mask: int32 [8, 512], P('dp'), may hold values 0 or 1
- position_index: int32 [16, 16], replicated, may hold values from 0 to 48
- out_cotangent: bfloat16 [4096, 512], P('dp'), may hold values from -6 to 6
Outputs:
- layer_out: float32 [4096, 512], P('dp')
- input_grad: float32 [4096, 512], P('dp')
- query_weight_grad: float32 [512, 512], P(None, 'tensor')
- key_weight_grad: float32 [512, 512], P(None, 'tensor')
- value_weight_grad: float32 [512, 512], P(None, 'tensor')
- query_bias_grad: float32 [512], P('tensor')
- value_bias_grad: float32 [512], P('tensor')
- position_bias_grad: float32 [49, 16], P(None, 'tensor')
- proj_weight_grad: float32 [512, 512], P('tensor')
- proj_bias_grad: float32 [512], replicated
- norm1_gain_grad: float32 [512], replicated
- norm1_shift_grad: float32 [512], replicated
- norm2_gain_grad: float32 [512], replicated
- norm2_shift_grad: float32 [512], replicated
- up_weight_grad: float32 [512, 2048], P(None, 'tensor')
- up_bias_grad: float32 [2048], P('tensor')
- down_weight_grad: float32 [2048, 512], P('tensor')
- down_bias_grad: float32 [512], replicated
Inputs may be any that keep to these rules, and one draw needn't show every extreme that they name: `segment_ids`: within each grid the clip numbers never fall, and each clip has 1 to 256 patches.
All inputs are finite; a program needn't handle non-finite values. No bound on the sum of `valid_mask` on one device may be relied on, other than what follows from the above.
Results may differ from a plain program's by a relative error of at most 0.012.
Values may be sent and summed in bfloat16 or wider, within the bound.
No kernel may reach another device: no remote copies, remote signals or barrier semaphores. Data moves between devices by JAX's collectives and lax.ppermute only.
A program may use at most 64 MiB of HBM per device.

v0:
```python
import jax
import jax.numpy as jnp
from jax import lax
from jax.sharding import PartitionSpec as P

HD = 32
GH = 64
GW = 8
WS = 4
NEG_FILL = -1e30


def normalize(value):
    centre = value - jnp.mean(value, axis=-1, keepdims=True)
    spread = jnp.mean(centre * centre, axis=-1, keepdims=True)
    inverse = lax.rsqrt(spread + 1e-06)
    return (centre * inverse, inverse)


def norm_back(grad_out, normed, inverse, gain):
    scaled = grad_out * gain
    first_mean = jnp.mean(scaled, axis=-1, keepdims=True)
    second_mean = jnp.mean(scaled * normed, axis=-1, keepdims=True)
    return inverse * (scaled - first_mean - normed * second_mean)


def to_windows(field):
    grids = field.shape[0] // (GH * GW)
    chans = field.shape[-1]
    shaped = field.reshape(grids, GH // WS, WS, GW // WS, WS, chans)
    return shaped.transpose(0, 1, 3, 2, 4, 5).reshape(-1, WS * WS, chans)


def from_windows(field):
    chans = field.shape[-1]
    grids = field.shape[0] // (GH // WS * (GW // WS))
    shaped = field.reshape(grids, GH // WS, GW // WS, WS, WS, chans)
    return shaped.transpose(0, 1, 3, 2, 4, 5).reshape(-1, chans)


def matmul(left, right):
    return jnp.dot(left, right, preferred_element_type=jnp.float32)


def gelu_fn(value):
    return jax.nn.gelu(value, approximate=True)


def tensor_reduce(col_grads, row_grads, small_grads):
    return (col_grads, row_grads, small_grads)


def shards(
    inputs,
    query_weight,
    key_weight,
    value_weight,
    query_bias,
    value_bias,
    position_bias,
    proj_weight,
    proj_bias,
    norm1_gain,
    norm1_shift,
    norm2_gain,
    norm2_shift,
    up_weight,
    up_bias,
    down_weight,
    down_bias,
    segment_ids,
    valid_mask,
    position_index,
    out_cotangent,
):
    window = WS * WS
    factor = HD ** (-0.5)
    width = inputs.shape[1]
    x_rows = to_windows(inputs).reshape(-1, width)
    cot_rows = to_windows(out_cotangent).reshape(-1, width)
    seg_rows = to_windows(segment_ids.reshape(-1, 1)).reshape(-1)
    valid_rows = to_windows(valid_mask.reshape(-1, 1)).reshape(-1)
    wq, wk, wv, w_up = (query_weight, key_weight, value_weight, up_weight)
    w_proj, w_down = (proj_weight, down_weight)
    b_query, b_value, b_up, rel_bias = (query_bias, value_bias, up_bias, position_bias)
    local_heads = wq.shape[1] // HD
    xfull = x_rows.astype(jnp.float32)
    normed1, inverse1 = normalize(xfull)
    first = (normed1 * norm1_gain + norm1_shift).astype(jnp.bfloat16)
    query = (matmul(first, wq) + b_query).astype(jnp.bfloat16)
    key = matmul(first, wk).astype(jnp.bfloat16)
    value = (matmul(first, wv) + b_value).astype(jnp.bfloat16)
    qwin = query.reshape(-1, window, local_heads, HD)
    kwin = key.reshape(-1, window, local_heads, HD)
    vwin = value.reshape(-1, window, local_heads, HD)
    offsets = lax.broadcasted_iota(jnp.int32, (window * window, rel_bias.shape[0]), 1)
    onehot = (position_index.reshape(-1, 1) == offsets).astype(jnp.float32)
    bias = jnp.dot(onehot, rel_bias, precision=lax.Precision.HIGHEST)
    bias = bias.reshape(window, window, local_heads).transpose(2, 0, 1)
    segwin = seg_rows.reshape(-1, window)
    validwin = valid_rows.reshape(-1, window)
    selfs = jnp.eye(window, dtype=jnp.int32) > 0
    allowed = (segwin[:, :, None] == segwin[:, None, :]) & (
        (validwin[:, None, :] > 0) | selfs[None]
    )
    scores = (
        jnp.einsum("wqhd,wkhd->whqk", qwin, kwin, preferred_element_type=jnp.float32) * factor
        + bias[None]
    )
    scores = jnp.where(allowed[:, None], scores, NEG_FILL)
    top = jnp.max(scores, axis=-1, keepdims=True)
    expo = jnp.exp(scores - top)
    probs = expo / jnp.sum(expo, axis=-1, keepdims=True)
    probs_low = probs.astype(jnp.bfloat16)
    attended = jnp.einsum("whqk,wkhd->wqhd", probs_low, vwin, preferred_element_type=jnp.float32)
    attended = attended.reshape(-1, local_heads * HD).astype(jnp.bfloat16)
    attn_out = lax.psum(matmul(attended, w_proj), "tensor")
    mid = xfull + attn_out + proj_bias
    normed2, inverse2 = normalize(mid)
    second = (normed2 * norm2_gain + norm2_shift).astype(jnp.bfloat16)
    pre = matmul(second, w_up) + b_up
    hidden_full, gelu_pull = jax.vjp(gelu_fn, pre)
    hidden = hidden_full.astype(jnp.bfloat16)
    mlp_out = lax.psum(matmul(hidden, w_down).astype(jnp.bfloat16), "tensor").astype(jnp.float32)
    layer_rows = mid + mlp_out + down_bias
    grad_out = cot_rows.astype(jnp.float32)
    down_bias_grad = jnp.sum(grad_out, axis=0)
    grad_mlp = grad_out.astype(jnp.bfloat16)
    down_weight_grad = matmul(hidden.T, grad_mlp)
    grad_hidden = matmul(grad_mlp, w_down.T)
    grad_pre = gelu_pull(grad_hidden)[0].astype(jnp.bfloat16)
    up_bias_grad = jnp.sum(grad_pre.astype(jnp.float32), axis=0)
    up_weight_grad = matmul(second.T, grad_pre)
    grad_second = lax.psum(matmul(grad_pre, w_up.T), "tensor")
    norm2_gain_grad = jnp.sum(grad_second * normed2, axis=0)
    norm2_shift_grad = jnp.sum(grad_second, axis=0)
    grad_mid = grad_out + norm_back(grad_second, normed2, inverse2, norm2_gain)
    proj_bias_grad = jnp.sum(grad_mid, axis=0)
    grad_proj = grad_mid.astype(jnp.bfloat16)
    proj_weight_grad = matmul(attended.T, grad_proj)
    grad_att = matmul(grad_proj, w_proj.T).astype(jnp.bfloat16)
    gwin = grad_att.reshape(-1, window, local_heads, HD)
    grad_probs = jnp.einsum("wqhd,wkhd->whqk", gwin, vwin, preferred_element_type=jnp.float32)
    grad_value = jnp.einsum(
        "whqk,wqhd->wkhd", probs_low, gwin, preferred_element_type=jnp.float32
    ).astype(jnp.bfloat16)
    grad_scores = probs * (grad_probs - jnp.sum(probs * grad_probs, axis=-1, keepdims=True))
    grad_scores = grad_scores.astype(jnp.bfloat16)
    grad_query = (
        factor
        * jnp.einsum("whqk,wkhd->wqhd", grad_scores, kwin, preferred_element_type=jnp.float32)
    ).astype(jnp.bfloat16)
    grad_key = (
        factor
        * jnp.einsum("whqk,wqhd->wkhd", grad_scores, qwin, preferred_element_type=jnp.float32)
    ).astype(jnp.bfloat16)
    score_total = jnp.sum(grad_scores.astype(jnp.float32), axis=0)
    score_total = score_total.transpose(1, 2, 0).reshape(window * window, local_heads)
    position_bias_grad = jnp.dot(onehot.T, score_total, precision=lax.Precision.HIGHEST)
    query_rows = grad_query.reshape(-1, local_heads * HD)
    key_rows = grad_key.reshape(-1, local_heads * HD)
    value_rows = grad_value.reshape(-1, local_heads * HD)
    query_bias_grad = jnp.sum(query_rows.astype(jnp.float32), axis=0)
    value_bias_grad = jnp.sum(value_rows.astype(jnp.float32), axis=0)
    query_weight_grad = matmul(first.T, query_rows)
    key_weight_grad = matmul(first.T, key_rows)
    value_weight_grad = matmul(first.T, value_rows)
    first_part = matmul(query_rows, wq.T) + matmul(key_rows, wk.T) + matmul(value_rows, wv.T)
    grad_first = lax.psum(first_part, "tensor")
    norm1_gain_grad = jnp.sum(grad_first * normed1, axis=0)
    norm1_shift_grad = jnp.sum(grad_first, axis=0)
    grad_rows_out = grad_mid + norm_back(grad_first, normed1, inverse1, norm1_gain)
    (
        (wq_part, wk_part, wv_part, rel_part, w1_part),
        (bq_part, bv_part, wo_part, b1_part, w2_part),
        (bo_part, g1_part, s1_part, b2_part, g2_part, s2_part),
    ) = tensor_reduce(
        (query_weight_grad, key_weight_grad, value_weight_grad, position_bias_grad, up_weight_grad),
        (query_bias_grad, value_bias_grad, proj_weight_grad, up_bias_grad, down_weight_grad),
        (
            proj_bias_grad,
            norm1_gain_grad,
            norm1_shift_grad,
            down_bias_grad,
            norm2_gain_grad,
            norm2_shift_grad,
        ),
    )
    every = lax.psum(
        (
            wq_part,
            wk_part,
            wv_part,
            bq_part,
            bv_part,
            rel_part,
            wo_part,
            bo_part,
            g1_part,
            s1_part,
            w1_part,
            b1_part,
            w2_part,
            b2_part,
            g2_part,
            s2_part,
        ),
        "dp",
    )
    early_set = every[:10]
    late_set = every[10:]
    layer_out = from_windows(layer_rows.reshape(-1, window, width))
    input_grad = from_windows(grad_rows_out.reshape(-1, window, width))
    (
        wq_total,
        wk_total,
        wv_total,
        bq_total,
        bv_total,
        rel_total,
        wo_total,
        bo_total,
        g1_total,
        s1_total,
    ) = early_set
    w1_total, b1_total, w2_total, b2_total, g2_total, s2_total = late_set
    return (
        layer_out,
        input_grad,
        wq_total,
        wk_total,
        wv_total,
        bq_total,
        bv_total,
        rel_total,
        wo_total,
        bo_total,
        g1_total,
        s1_total,
        g2_total,
        s2_total,
        w1_total,
        b1_total,
        w2_total,
        b2_total,
    )


def solution(mesh):
    return jax.shard_map(
        shards,
        mesh=mesh,
        in_specs=(
            P("dp", None),
            P(None, "tensor"),
            P(None, "tensor"),
            P(None, "tensor"),
            P("tensor"),
            P("tensor"),
            P(None, "tensor"),
            P("tensor", None),
            P(),
            P(),
            P(),
            P(),
            P(),
            P(None, "tensor"),
            P("tensor"),
            P("tensor", None),
            P(),
            P("dp", None),
            P("dp", None),
            P(),
            P("dp", None),
        ),
        out_specs=(
            P("dp", None),
            P("dp", None),
            P(None, "tensor"),
            P(None, "tensor"),
            P(None, "tensor"),
            P("tensor"),
            P("tensor"),
            P(None, "tensor"),
            P("tensor", None),
            P(),
            P(),
            P(),
            P(),
            P(),
            P(None, "tensor"),
            P("tensor"),
            P("tensor", None),
            P(),
        ),
        check_vma=False,
    )
```

profile of v0, /device:TPU:0, one launch (start us, length us, event | category | flops | bytes accessed | tf_op | source)
XLA Modules:
  0.0 360.2 jit_solution(3782836094382820206)
XLA Ops:
  7.8 1.4 reshape.268
  15.8 1.6 reshape.266
  20.2 2.0 reshape.254
  22.2 1.6 fusion.12
  26.8 2.8 fusion.44
  29.6 1.8 fusion.9
  39.8 1.4 fusion.50
  41.3 31.5 %all-reduce.8.cloned.1.call-done = f32[512,512]{1,0:T(8,128)} async-done(((f32[512,512]{1,0:T(8,128)}), f32[512,512]{1,0:T(8,128)}) %all-reduce.8.cloned.1.call-update) | async-done | bytes 1048592 | tf_op jit(solution)/shard_map/psum | solution.py:117
  72.7 1.4 fusion.43
  75.4 1.7 convert_reduce_fusion.1
  77.2 1.6 fusion.38
  78.7 1.4 fusion.51
  80.2 2.7 convolution_convert_fusion.1
  82.9 2.7 fusion.40
  85.9 30.9 %all-reduce.12.cloned.1.call-done = f32[512,512]{1,0:T(8,128)} async-done(((f32[512,512]{1,0:T(8,128)}), f32[512,512]{1,0:T(8,128)}) %all-reduce.12.cloned.1.call-update) | async-done | bytes 1048592 | tf_op jit(solution)/shard_map/psum | solution.py:134
  116.8 1.7 multiply_reduce_fusion
  118.6 34.2 %all-reduce.10.cloned.1.call-done = bf16[512,512]{1,0:T(8,128)(2,1)} async-done(((bf16[512,512]{1,0:T(8,128)(2,1)}), bf16[512,512]{1,0:T(8,128)(2,1)}) %all-reduce.10.cloned.1.call-update) | async-done | bytes 524304 | tf_op jit(solution)/shard_map/psum | solution.py:124
  152.8 3.0 fusion.42
  158.1 2.9 convert_reduce_fusion.3
  170.1 1.3 convolution_add_fusion
  176.6 2.5 reshape_reshape.15
  179.2 2.3 copy.105
  181.5 2.6 reshape.258
  184.3 23.4 %all-reduce.14.cloned.1.call-done = f32[512,512]{1,0:T(8,128)} async-done(((f32[512,512]{1,0:T(8,128)}), f32[512,512]{1,0:T(8,128)}) %all-reduce.14.cloned.1.call-update) | async-done | bytes 1048592 | tf_op jit(solution)/shard_map/psum | solution.py:169
  207.8 1.8 multiply_reduce_fusion.1
  209.6 1.3 multiply_add_fusion
  211.0 1.5 reshape_reshape.17
  212.6 1.3 reshape.264
  214.6 39.6 %all-reduce = (f32[128]{0:T(128)}, f32[128]{0:T(128)}, f32[49,4]{0,1:T(4,128)}, f32[512]{0:T(512)}, f32[512]{0:T(512)}, /*index=5*/f32[512]{0:T(512)}, f32[512]{...) all-reduce(f32[128]{0:T(128)S(1)} %reduce_sum.195, ...), channel_id=1, replica_groups=mesh['dp'=8,'tensor'=4] {'dp'}, use_global_device_ids=true, to_apply=%region_19.20 | all-reduce | flops 4036 | bytes 32288 | tf_op jit(solution)/shard_map/psum | solution.py:189
  254.2 91.6 %all-reduce.16.cloned.1.call-done = (f32[512,128]{1,0:T(8,128)}, f32[512,128]{1,0:T(8,128)}, f32[512,128]{1,0:T(8,128)}, f32[128,512]{1,0:T(8,128)}, f32[512,512]{1,0:T(8,128)}, /*index=5*/f32[512,512]{1,0:T(8,128)}) async-done(((f32[512,128]{1,0:T(8,128)}, f32[512,128]{1,0:T(8,128)}, f32[512,128]{1,0:T(8,128)}, f32[128,512]{1,0:T(8,128)}, f32[512,512]{1,0:T(8,128)}, /*index=5*/f32[512,512]{1,0:T(8,128)}), ...) | async-done | bytes 3145744 | tf_op jit(solution)/shard_map/psum | solution.py:189
  345.9 1.8 copy.170
  347.6 1.7 copy.171
  (196 shorter events, 44.6 us)
Async XLA Ops:
  7.2 67.3 %copy-start = (bf16[512,512]{1,0:T(8,128)(2,1)S(1)}, bf16[512,512]{1,0:T(8,128)(2,1)}, u32[]{:S(2)}) copy-start(bf16[512,512]{1,0:T(8,128)(2,1)} %param.34) | copy-start | bytes 1572868
  7.2 65.5 %all-reduce.8.cloned.1.call-start = ((), (), s32[]{:S(2)}) async-start(), calls=%async_computation | async-start | bytes 2097152 | tf_op jit(solution)/shard_map/psum | solution.py:117
  9.6 7.8 %copy-start.33 = (f32[512]{0:T(512)}, f32[512]{0:T(512)S(1)}, u32[]{:S(2)}) copy-start(f32[512]{0:T(512)S(1)} %div.35) | copy-start | bytes 6148
  13.5 1.2 copy-start.51
  15.8 1.6 copy-start.35
  15.8 1.6 copy-start.31
  15.8 1.6 copy-start.40
  20.2 2.0 copy-start.19
  25.0 4.6 %copy-start.8 = (bf16[32,16,4,32]{3,2,1,0:T(4,128)(2,1)}, bf16[32,16,4,32]{3,2,1,0:T(4,128)(2,1)S(1)}, u32[]{:S(2)}) copy-start(bf16[32,16,4,32]{3,2,1,0:T(4,128)(2,1)S(1)} %reshape.255) | copy-start | bytes 393220
  29.6 1.8 copy-start.29
  33.8 83.0 %all-reduce.12.cloned.1.call-start = ((), (), s32[]{:S(2)}) async-start(), calls=%async_computation.2 | async-start | bytes 2097152 | tf_op jit(solution)/shard_map/psum | solution.py:134
  37.3 2.5 copy-start.5
  38.6 1.2 copy-start.25
  39.8 32.9 %copy-start.44 = (f32[512]{0:T(512)S(1)}, f32[512]{0:T(512)}, u32[]{:S(2)}) copy-start(f32[512]{0:T(512)} %param.29) | copy-start | bytes 6148
  75.4 1.8 copy-start.6
  77.1 1.6 copy-start.57
  77.2 1.6 copy-start.10
  80.2 72.6 %all-reduce.10.cloned.1.call-start = ((), (), s32[]{:S(2)}) async-start(), calls=%async_computation.1 | async-start | bytes 1048576 | tf_op jit(solution)/shard_map/psum | solution.py:124
  85.7 122.1 %all-reduce.14.cloned.1.call-start = ((), (), s32[]{:S(2)}) async-start(), calls=%async_computation.3 | async-start | bytes 2097152 | tf_op jit(solution)/shard_map/psum | solution.py:169
  118.6 34.2 %copy-start.46 = (f32[512]{0:T(512)S(1)}, f32[512]{0:T(512)}, u32[]{:S(2)}) copy-start(f32[512]{0:T(512)} %param.37) | copy-start | bytes 6148
  155.8 2.3 copy-start.11
  158.1 2.9 copy-start.17
  158.1 2.9 copy-start.18
  171.5 2.1 copy-start.2
  171.5 174.4 %all-reduce.16.cloned.1.call-start = ((), (), s32[]{:S(2)}) async-start(), calls=%async_computation.4 | async-start | bytes 6291456 | tf_op jit(solution)/shard_map/psum | solution.py:189
  181.5 2.6 copy-start.53
  184.1 23.7 %copy-start.34 = (f32[512]{0:T(512)S(1)}, f32[512]{0:T(512)}, u32[]{:S(2)}) copy-start(f32[512]{0:T(512)} %copy-done.33) | copy-start | bytes 6148
  184.1 23.7 %copy-start.36 = (f32[512]{0:T(512)S(1)}, f32[512]{0:T(512)}, u32[]{:S(2)}) copy-start(f32[512]{0:T(512)} %copy-done.35) | copy-start | bytes 6148
  207.8 1.8 copy-start.7
  345.9 3.4 copy-start.27
  345.9 5.2 %copy-start.13 = (f32[512,512]{1,0:T(8,128)S(1)}, f32[512,512]{1,0:T(8,128)}, u32[]{:S(2)}) copy-start(f32[512,512]{1,0:T(8,128)} %get-tuple-element.76) | copy-start | bytes 3145732
  351.1 1.6 copy-start.12
  (31 other events, 30.0 us)
Sparse Core Ops, SparseCore 0:
  33.9 38.7 all-reduce.7
  80.3 36.4 all-reduce.11
  119.2 33.5 all-reduce.9
  171.6 36.1 all-reduce.13
  213.6 132.1 all-reduce.15
where the time goes:
time: 362 us; the launch traced here: 360 us
  waiting for transfers between devices  212 us (59%)
  local copies, waits for them, and re-layouts  47.8 us (13%)
  blocking collectives  39.6 us (11%)
  matrix products  31.7 us (9%)
  other arithmetic  14.5 us (4%)
  between operations  14.4 us (4%)
    psum x1, waiting for transfers between devices, shards(): lax.psum((wq_part, wk_part, wv_part, bq_part, bv_part, rel_part, wo_part,...  91.6 us
    psum x1, blocking collectives, shards(): lax.psum((wq_part, wk_part, wv_part, bq_part, bv_part, rel_part, wo_part,...  39.6 us
    psum x1, waiting for transfers between devices, shards(): lax.psum(matmul(hidden, w_down).astype(jnp.bfloat16), 'tensor')  34.2 us
    psum x1, waiting for transfers between devices, shards(): attn_out = lax.psum(matmul(attended, w_proj), 'tensor')  31.5 us
    psum x1, waiting for transfers between devices, shards(): grad_second = lax.psum(matmul(grad_pre, w_up.T), 'tensor')  30.9 us
    psum x1, waiting for transfers between devices, shards(): grad_first = lax.psum(first_part, 'tensor')  23.4 us
    dot_general x18, matrix products, matmul(): return jnp.dot(left, right, preferred_element_type=jnp.float32)  22 us
    unnamed x123, local copies, waits for them, and re-layouts  17.8 us
  transfers between devices with their start and end apart: 5, of which 5 were waited for; matrix products, arithmetic and copies ran while one was open for 9% of the time, Pallas kernels for 0%

commit v1 on v0

--- a/solution.py
+++ b/solution.py
@@ -1,3 +1,4 @@
+import functools
 import jax
 import jax.numpy as jnp
 from jax import lax
@@ -8,6 +9,14 @@
 GW = 8
 WS = 4
 NEG_FILL = -1e30
+
+
+def surface_spread(content, mesh_ax):
+    local_now = lax.all_gather(content, mesh_ax)
+    return jnp.sum(local_now, axis=0)
+
+
+lift_streams = functools.partial(surface_spread, mesh_ax="tensor")
 
 
 def normalize(value):
@@ -121,7 +130,7 @@
     pre = matmul(second, w_up) + b_up
     hidden_full, gelu_pull = jax.vjp(gelu_fn, pre)
     hidden = hidden_full.astype(jnp.bfloat16)
-    mlp_out = lax.psum(matmul(hidden, w_down).astype(jnp.bfloat16), "tensor").astype(jnp.float32)
+    mlp_out = lift_streams(matmul(hidden, w_down).astype(jnp.bfloat16)).astype(jnp.float32)
     layer_rows = mid + mlp_out + down_bias
     grad_out = cot_rows.astype(jnp.float32)
     down_bias_grad = jnp.sum(grad_out, axis=0)

time: 362 us -> 354 us (0.978)
  waiting for transfers between devices: 212 us -> 198 us
  matrix products: 31.7 us -> 37.6 us
  local copies, waits for them, and re-layouts: 47.8 us -> 43 us
  other arithmetic: 14.5 us -> 19 us
    psum x1 -> x0, waiting for transfers between devices: 34.2 us -> none  [shards(): lax.psum(matmul(hidden, w_down).astype(jnp.bfloat16), 'tensor')]
    all_gather x0 -> x1, waiting for transfers between devices: none -> 22.8 us  [surface_spread(): local_now = lax.all_gather(content, mesh_ax)]
    unnamed x123 -> x107, local copies, waits for them, and re-layouts: 17.8 us -> 11.7 us
    dot_general x18, matrix products: 22 us -> 26.9 us  [matmul(): return jnp.dot(left, right, preferred_element_type=jnp.float32)]
    psum x1, waiting for transfers between devices: 30.9 us -> 26.5 us  [shards(): grad_second = lax.psum(matmul(grad_pre, w_up.T), 'tensor')]
  transfers between devices with their start and end apart: 5 -> 5, of which waited for: 5 -> 5; matrix products, arithmetic and copies ran while one was open for 9% -> 10% of each run, Pallas kernels for 0% -> 0%
where the time goes in v1:
time: 354 us; the launch traced here: 352 us
  waiting for transfers between devices  198 us (56%)
  local copies, waits for them, and re-layouts  43 us (12%)
  blocking collectives  39.7 us (11%)
  matrix products  37.6 us (11%)
  other arithmetic  19 us (5%)
  between operations  14.5 us (4%)
    psum x1, waiting for transfers between devices, shards(): lax.psum((wq_part, wk_part, wv_part, bq_part, bv_part, rel_part, wo_part,...  92.4 us
    psum x1, blocking collectives, shards(): lax.psum((wq_part, wk_part, wv_part, bq_part, bv_part, rel_part, wo_part,...  39.7 us
    psum x1, waiting for transfers between devices, shards(): attn_out = lax.psum(matmul(attended, w_proj), 'tensor')  32.1 us
    dot_general x18, matrix products, matmul(): return jnp.dot(left, right, preferred_element_type=jnp.float32)  26.9 us
    psum x1, waiting for transfers between devices, shards(): grad_second = lax.psum(matmul(grad_pre, w_up.T), 'tensor')  26.5 us
    psum x1, waiting for transfers between devices, shards(): grad_first = lax.psum(first_part, 'tensor')  24.4 us
    all_gather x1, waiting for transfers between devices, surface_spread(): local_now = lax.all_gather(content, mesh_ax)  22.8 us
    unnamed x107, local copies, waits for them, and re-layouts  11.7 us
  transfers between devices with their start and end apart: 5, of which 5 were waited for; matrix products, arithmetic and copies ran while one was open for 10% of the time, Pallas kernels for 0%

profile of v1, /device:TPU:0, one launch (start us, length us, event | category | flops | bytes accessed | tf_op | source)
XLA Modules:
  0.0 352.5 jit_solution(9671133157634487677)
XLA Ops:
  16.1 1.6 reshape.266
  20.7 2.0 reshape.254
  22.6 1.6 fusion.12
  27.4 2.8 fusion.44
  30.2 1.8 fusion.9
  36.1 2.0 reshape_reshape.16
  38.1 2.6 fusion.50
  40.7 32.1 %all-reduce.7.cloned.1.call-done = f32[512,512]{1,0:T(8,128)} async-done(((f32[512,512]{1,0:T(8,128)}), f32[512,512]{1,0:T(8,128)}) %all-reduce.7.cloned.1.call-update) | async-done | bytes 1048592 | tf_op jit(solution)/shard_map/psum | solution.py:126
  72.8 1.5 fusion.43
  74.6 2.7 convert_reduce_fusion.1
  79.7 2.5 convolution_convert_fusion.1
  85.0 3.0 fusion.38
  88.0 1.7 fusion.40
  89.7 26.5 %all-reduce.9.cloned.1.call-done = f32[512,512]{1,0:T(8,128)} async-done(((f32[512,512]{1,0:T(8,128)}), f32[512,512]{1,0:T(8,128)}) %all-reduce.9.cloned.1.call-update) | async-done | bytes 1048592 | tf_op jit(solution)/shard_map/psum | solution.py:143
  116.2 1.7 multiply_reduce_fusion
  117.9 22.8 %all-gather.3.cloned.1.call-done = bf16[2048,512]{1,0:T(8,128)(2,1)} async-done(((bf16[512,512]{1,0:T(8,128)(2,1)}), bf16[2048,512]{1,0:T(8,128)(2,1)}) %all-gather.3.cloned.1.call-update) | async-done | bytes 2097168 | tf_op jit(solution)/shard_map/all_gather | solution.py:15
  140.7 2.9 reduce_sum.201
  143.6 3.0 fusion.42
  148.2 3.1 convert_reduce_fusion.3
  153.3 1.7 convert_reduce_fusion.4
  166.7 2.5 reshape_reshape.15
  169.2 2.4 copy.105
  171.6 2.6 reshape.258
  174.4 24.4 %all-reduce.11.cloned.1.call-done = f32[512,512]{1,0:T(8,128)} async-done(((f32[512,512]{1,0:T(8,128)}), f32[512,512]{1,0:T(8,128)}) %all-reduce.11.cloned.1.call-update) | async-done | bytes 1048592 | tf_op jit(solution)/shard_map/psum | solution.py:178
  198.8 1.8 multiply_reduce_fusion.1
  202.0 1.5 reshape_reshape.17
  205.1 39.7 %all-reduce = (f32[128]{0:T(128)}, f32[128]{0:T(128)}, f32[49,4]{0,1:T(4,128)}, f32[512]{0:T(512)}, f32[512]{0:T(512)}, /*index=5*/f32[512]{0:T(512)}, f32[512]{...) all-reduce(f32[128]{0:T(128)S(1)} %reduce_sum.208, ...), channel_id=1, replica_groups=mesh['dp'=8,'tensor'=4] {'dp'}, use_global_device_ids=true, to_apply=%region_19.20 | all-reduce | flops 4036 | bytes 32288 | tf_op jit(solution)/shard_map/psum | solution.py:198
  244.7 92.4 %all-reduce.13.cloned.1.call-done = (f32[512,128]{1,0:T(8,128)}, f32[512,128]{1,0:T(8,128)}, f32[512,128]{1,0:T(8,128)}, f32[128,512]{1,0:T(8,128)}, f32[512,512]{1,0:T(8,128)}, /*index=5*/f32[512,512]{1,0:T(8,128)}) async-done(((f32[512,128]{1,0:T(8,128)}, f32[512,128]{1,0:T(8,128)}, f32[512,128]{1,0:T(8,128)}, f32[128,512]{1,0:T(8,128)}, f32[512,512]{1,0:T(8,128)}, /*index=5*/f32[512,512]{1,0:T(8,128)}), ...) | async-done | bytes 3145744 | tf_op jit(solution)/shard_map/psum | solution.py:198
  337.2 1.8 copy.169
  339.0 1.7 copy.170
  340.7 1.7 copy.171
  342.3 1.7 copy.172
  (181 shorter events, 44.3 us)
Async XLA Ops:
  7.2 67.4 %copy-start = (bf16[512,512]{1,0:T(8,128)(2,1)S(1)}, bf16[512,512]{1,0:T(8,128)(2,1)}, u32[]{:S(2)}) copy-start(bf16[512,512]{1,0:T(8,128)(2,1)} %param.34) | copy-start | bytes 1572868
  7.2 65.6 %all-reduce.7.cloned.1.call-start = ((), (), s32[]{:S(2)}) async-start(), calls=%async_computation | async-start | bytes 2097152 | tf_op jit(solution)/shard_map/psum | solution.py:126
  9.5 4.9 %copy-start.44 = (s32[1,512]{1,0:T(1,128)S(1)}, s32[1,512]{1,0:T(1,128)}, u32[]{:S(2)}) copy-start(s32[1,512]{1,0:T(1,128)} %param.38) | copy-start | bytes 6148
  13.2 5.6 %copy-start.23 = (bf16[512,128]{1,0:T(8,128)(2,1)S(1)}, bf16[512,128]{1,0:T(8,128)(2,1)}, u32[]{:S(2)}) copy-start(bf16[512,128]{1,0:T(8,128)(2,1)} %param.23) | copy-start | bytes 393220
  17.7 4.9 %copy-start.22 = (bf16[512,128]{1,0:T(8,128)(2,1)S(1)}, bf16[512,128]{1,0:T(8,128)(2,1)}, u32[]{:S(2)}) copy-start(bf16[512,128]{1,0:T(8,128)(2,1)} %param.22) | copy-start | bytes 393220
  19.7 5.7 %copy-start.26 = (bf16[512,128]{1,0:T(8,128)(2,1)S(1)}, bf16[512,128]{1,0:T(8,128)(2,1)}, u32[]{:S(2)}) copy-start(bf16[512,128]{1,0:T(8,128)(2,1)} %convolution_convert_fusion.4) | copy-start | bytes 393220
  25.4 4.7 %copy-start.8 = (bf16[32,16,4,32]{3,2,1,0:T(4,128)(2,1)}, bf16[32,16,4,32]{3,2,1,0:T(4,128)(2,1)S(1)}, u32[]{:S(2)}) copy-start(bf16[32,16,4,32]{3,2,1,0:T(4,128)(2,1)S(1)} %reshape.255) | copy-start | bytes 393220
  32.5 3.6 %copy-start.12 = (bf16[512,128]{1,0:T(8,128)(2,1)}, bf16[512,128]{1,0:T(8,128)(2,1)S(1)}, u32[]{:S(2)}) copy-start(bf16[512,128]{1,0:T(8,128)(2,1)S(1)} %convert_element_type.138) | copy-start | bytes 393220
  33.8 82.4 %all-reduce.9.cloned.1.call-start = ((), (), s32[]{:S(2)}) async-start(), calls=%async_computation.1 | async-start | bytes 2097152 | tf_op jit(solution)/shard_map/psum | solution.py:143
  35.0 5.7 %copy-start.5 = (bf16[1,16,4,2,4,512]{5,4,3,2,1,0:T(4,128)(2,1)}, bf16[1,16,4,2,4,512]{5,4,3,2,1,0:T(4,128)(2,1)S(1)}, u32[]{:S(2)}) copy-start(bf16[1,16,4,2,4,512]{5,4,3,2,1,0:T(4,128)(2,1)S(1)} %reshape.259) | copy-start | bytes 1572868
  35.0 37.7 %copy-start.37 = (f32[512]{0:T(512)S(1)}, f32[512]{0:T(512)}, u32[]{:S(2)}) copy-start(f32[512]{0:T(512)} %param.29) | copy-start | bytes 6148
  40.7 33.9 %copy-start.34 = (f32[512]{0:T(512)S(1)}, f32[512]{0:T(512)}, u32[]{:S(2)}) copy-start(f32[512]{0:T(512)} %param.32) | copy-start | bytes 6148
  40.7 33.9 %copy-start.38 = (f32[512]{0:T(512)S(1)}, f32[512]{0:T(512)}, u32[]{:S(2)}) copy-start(f32[512]{0:T(512)} %param.33) | copy-start | bytes 6148
  40.7 33.9 %copy-start.49 = (f32[512]{0:T(512)S(1)}, f32[512]{0:T(512)}, u32[]{:S(2)}) copy-start(f32[512]{0:T(512)} %param.35) | copy-start | bytes 6148
  74.3 3.0 copy-start.1
  79.6 61.1 %all-gather.3.cloned.1.call-start = ((), (), s32[]{:S(2)}) async-start(), calls=%async_computation.3 | async-start | bytes 2621440 | tf_op jit(solution)/shard_map/all_gather | solution.py:15
  82.2 116.6 %all-reduce.11.cloned.1.call-start = ((), (), s32[]{:S(2)}) async-start(), calls=%async_computation.2 | async-start | bytes 2097152 | tf_op jit(solution)/shard_map/psum | solution.py:178
  83.7 4.3 %copy-start.2 = (f32[512,512]{1,0:T(8,128)S(1)}, f32[512,512]{1,0:T(8,128)}, u32[]{:S(2)}) copy-start(f32[512,512]{1,0:T(8,128)} %copy-done.1) | copy-start | bytes 3145732
  85.0 3.0 copy-start.11
  89.7 53.9 %copy-start.39 = (f32[512]{0:T(512)S(1)}, f32[512]{0:T(512)}, u32[]{:S(2)}) copy-start(f32[512]{0:T(512)} %param.37) | copy-start | bytes 6148
  143.6 4.5 %copy-start.30 = (f32[32,4,16]{2,1,0:T(4,128)S(1)}, f32[32,4,16]{2,1,0:T(4,128)}, u32[]{:S(2)}) copy-start(f32[32,4,16]{2,1,0:T(4,128)} %copy-done.29) | copy-start | bytes 24580
  148.1 3.2 copy-start.14
  148.1 3.1 copy-start.20
  157.7 3.5 copy-start.25
  161.2 3.5 copy-start.4
  161.2 3.5 copy-start.13
  162.6 174.6 %all-reduce.13.cloned.1.call-start = ((), (), s32[]{:S(2)}) async-start(), calls=%async_computation.4 | async-start | bytes 6291456 | tf_op jit(solution)/shard_map/psum | solution.py:198
  169.2 4.9 %copy-start.46 = (s32[256]{0:T(256)S(1)}, s32[256]{0:T(256)}, u32[]{:S(2)}) copy-start(s32[256]{0:T(256)} %copy-done.45) | copy-start | bytes 3076
  169.2 29.6 %copy-start.32 = (f32[512]{0:T(512)S(1)}, f32[512]{0:T(512)}, u32[]{:S(2)}) copy-start(f32[512]{0:T(512)} %div.35) | copy-start | bytes 6148
  169.2 29.6 %copy-start.33 = (f32[512]{0:T(512)S(1)}, f32[512]{0:T(512)}, u32[]{:S(2)}) copy-start(f32[512]{0:T(512)} %rsqrt.21) | copy-start | bytes 6148
  337.2 6.8 %copy-start.16 = (f32[512,512]{1,0:T(8,128)S(1)}, f32[512,512]{1,0:T(8,128)}, u32[]{:S(2)}) copy-start(f32[512,512]{1,0:T(8,128)} %get-tuple-element.76) | copy-start | bytes 3145732
  337.2 7.8 %copy-start.15 = (f32[512,512]{1,0:T(8,128)S(1)}, f32[512,512]{1,0:T(8,128)}, u32[]{:S(2)}) copy-start(f32[512,512]{1,0:T(8,128)} %get-tuple-element.78) | copy-start | bytes 3145732
  (23 other events, 40.3 us)
Sparse Core Ops, SparseCore 0:
  33.9 38.8 all-reduce.6
  79.7 36.4 all-reduce.8
  117.7 22.9 all-gather.2
  162.7 36.0 all-reduce.10
  204.7 132.4 all-reduce.12
